TPU v7x, 512 devices: a whole 4x8x8 slice. The times are simulated.
512 devices in a mesh: chan: 64 (over z, y_lo, x), facet: 8 (over y_hi, core).
Axes of the slice: x: 4, y: 8 (y_hi: 4, y_lo: 2; y = y_hi * 2 + y_lo), z: 8, core: 2. Of those that a mesh axis runs over, the one named last changes fastest.
Arguments:
- estimate: float32 [256, 128, 1024], P('chan', None, 'facet'), may hold values from -16 to 16
- dirty: float32 [256, 128, 1024], P('chan', None, 'facet'), may hold values from -16 to 16
- weights: float32 [256, 128, 1024], P('chan', None, 'facet'), may hold values from 0.2 to 1
- margin: int32 [8], replicated, may hold values from 1 to 16, as said below
- blend_table: int32 [8, 160], replicated, may hold values from 1 to 8
- tau_steps: int32 [2], replicated, may hold values from 1 to 4
Outputs:
- updated: float32 [256, 128, 1024], P('chan', None, 'facet')
Inputs may be any that keep to these rules, and one draw needn't show every extreme that they name: Some facet has margin exactly 16.
All inputs are finite; a program needn't handle non-finite values.
Results may differ from a plain program's by a relative error of at most 0.00012.
Values sent between devices are 32-bit elements; how exact they have to be, the bound alone decides.
No kernel may reach another device: no remote copies, remote signals or barrier semaphores. Data moves between devices by JAX's collectives and lax.ppermute only.
A program may use at most 64 MiB of HBM per device.

v0:
```python
import math
import jax
import jax.numpy as jnp
from jax import lax
from jax.sharding import PartitionSpec as P

OV = 16
NS_STEPS = 2
ITERS = 2


def padded(shard, sides, width):
    for axis, dim in sides:
        size, length = (lax.axis_size(axis), shard.shape[dim])
        up = [(i, (i + 1) % size) for i in range(size - 1)]
        down = [(j, i) for i, j in up]
        last = lax.slice_in_dim(shard, length - width, length, axis=dim)
        initial = lax.slice_in_dim(shard, 0, width, axis=dim)
        before = lax.ppermute(last, axis, up)
        after = lax.ppermute(initial, axis, down)
        shard = jnp.concatenate([before, shard, after], axis=dim)
    return shard


def apply_shrink(gram, columns, tau_value):
    channel_count = gram.shape[0]
    identity = jnp.eye(channel_count, dtype=jnp.float32)
    mean_eigen = jnp.trace(gram) / channel_count + 1e-06
    target = (gram + 0.01 * mean_eigen * identity) / (16.16 * mean_eigen)
    inverse_root = identity
    for newton_step in range(NS_STEPS):
        middle = 1.5 * identity - 0.5 * jnp.dot(
            inverse_root, target, precision=lax.Precision.HIGHEST
        )
        target = jnp.dot(target, middle, precision=lax.Precision.HIGHEST)
        inverse_root = jnp.dot(middle, inverse_root, precision=lax.Precision.HIGHEST)
    factor = 0.1 * tau_value / math.sqrt(1.01)
    kernel = identity - factor * inverse_root
    return jnp.dot(kernel, columns, precision=lax.Precision.HIGHEST)


def shrink_block(block, tau_value):
    columns = block.reshape(block.shape[0], -1)
    partial_value = jnp.dot(columns, columns.T, precision=lax.Precision.HIGHEST)
    gram = lax.psum(partial_value, "chan")
    return apply_shrink(gram, columns, tau_value).reshape(block.shape)


def extend(moved_cube):
    return padded(moved_cube, (("facet", 2),), OV)


def blend_sums(margin, blend_table, facet_id, facet_total, center):
    center_index = jnp.arange(center, dtype=jnp.int32)
    table_float = blend_table.astype(jnp.float32)
    own_part = table_float[facet_id][OV : OV + center]
    before_id = jnp.maximum(facet_id - 1, 0)
    after_id = jnp.minimum(facet_id + 1, facet_total - 1)
    before_slice = jnp.pad(table_float[before_id][center + OV :], (0, center - OV))
    after_slice = jnp.pad(table_float[after_id][:OV], (center - OV, 0))
    before_ok = (facet_id > 0) & (center_index < margin[before_id])
    after_ok = (facet_id < facet_total - 1) & (center_index >= center - margin[after_id])
    return (
        own_part + jnp.where(before_ok, before_slice, 0.0) + jnp.where(after_ok, after_slice, 0.0)
    )


def blend(result, row_weight, denominator, center):
    weighted = result * row_weight
    rims = jnp.concatenate([weighted[:, :, :OV], weighted[:, :, center + OV :]], axis=2)
    received = padded(rims, (("facet", 2),), OV)
    from_before = jnp.pad(received[:, :, :OV], ((0, 0), (0, 0), (0, center - OV)))
    from_after = jnp.pad(
        received[:, :, received.shape[2] - OV :], ((0, 0), (0, 0), (center - OV, 0))
    )
    core_rows = weighted[:, :, OV : OV + center] + from_before + from_after
    return core_rows / denominator


def per_device(estimate, dirty, weights, margin, blend_table, tau_steps):
    facet_id = lax.axis_index("facet")
    facet_total = lax.axis_size("facet")
    center = estimate.shape[2]
    ext_len = center + 2 * OV
    row_index = jnp.arange(ext_len, dtype=jnp.int32)
    own_width = margin[facet_id]
    keep_rows = ((row_index >= OV - own_width) & (row_index < center + OV + own_width)).astype(
        jnp.float32
    )
    row_weight = blend_table[facet_id].astype(jnp.float32) * keep_rows
    denominator = blend_sums(margin, blend_table, facet_id, facet_total, center)
    current = estimate
    for iteration in range(ITERS):
        tau_value = tau_steps[iteration].astype(jnp.float32)
        moved_cube = current - weights * (current - dirty)
        extended = extend(moved_cube) * keep_rows
        pixel_view = lax.all_to_all(extended, "chan", split_axis=1, concat_axis=0, tiled=True)
        result = shrink_block(pixel_view, tau_value)
        back_view = lax.all_to_all(result, "chan", split_axis=0, concat_axis=1, tiled=True)
        current = blend(back_view, row_weight, denominator, center)
    return current


def solution(mesh):
    placed = (
        P("chan", None, "facet"),
        P("chan", None, "facet"),
        P("chan", None, "facet"),
        P(),
        P(),
        P(),
    )
    return jax.shard_map(
        per_device, mesh=mesh, in_specs=placed, out_specs=P("chan", None, "facet"), check_vma=False
    )
```

profile of v0, /device:TPU:1, one launch (start us, length us, event | category | flops | bytes accessed | tf_op | source)
XLA Modules:
  0.0 1311.3 jit_solution(14268849020404267029)
XLA Ops:
  6.5 1.1 multiply_subtract_fusion.1
  7.8 5.6 collective-permute-start
  13.4 4.5 collective-permute-start.1
  17.9 0.6 copy-done.5
  18.6 0.7 fusion.28
  20.5 4.3 collective-permute-done.1
  25.1 0.3 copy.53
  25.4 26.8 %all_to_all.66 = f32[4,128,160]{2,0,1:T(4,128)S(1)} all-to-all(f32[4,128,160]{2,0,1:T(4,128)S(1)} %copy.53), channel_id=1, replica_groups=mesh['chan'=64,'facet'=8] {'chan'}, dimensions={1} | all-to-all | bytes 655360 | tf_op jit(solution)/shard_map/all_to_all | solution.py:97
  52.5 0.4 reshape.45
  53.0 1.3 fusion.29
  54.3 0.6 copy-done.6
  54.9 0.6 fusion.27
  56.3 531.9 %all-reduce.9.cloned.1.call-done = f32[256,256]{1,0:T(8,128)} async-done(((f32[256,256]{1,0:T(8,128)}), f32[256,256]{1,0:T(8,128)}) %all-reduce.9.cloned.1.call-update) | async-done | bytes 262160 | tf_op jit(solution)/shard_map/psum | solution.py:45
  588.3 1.7 select_reduce_fusion.1
  591.2 0.4 fusion.14
  591.6 0.4 fusion.6
  592.0 0.4 fusion.5
  592.4 0.5 fusion.30
  592.9 1.0 copy.56
  593.9 9.1 all-to-all-start.1
  603.1 0.6 copy-done.4
  604.5 11.8 all-to-all-done.1
  616.7 35.2 %collective-permute-start.2 = (f32[4,128,16]{2,1,0:T(8,128)S(1)}, f32[4,128,16]{2,1,0:T(8,128)S(1)}, u32[]{:S(2)}, u32[]{:S(2)}) collective-permute-start(f32[4,128,16]{2,1,0:T(8,128)S(1)} %get-tuple-element.7), channel_id=1, source_target_pairs={{0,1},{1,2},{2,3},{3,4},{4,5},{5,6},{6,7},{8,9},{9,10},{10,11},{11... | collective-permute-start | bytes 98312 | tf_op jit(solution)/shard_map/ppermute | solution.py:19
  651.9 1.9 collective-permute-start.3
  653.8 0.7 fusion.17
  654.5 0.7 collective-permute-done.2
  655.2 8.1 collective-permute-done.3
  663.6 1.9 collective-permute-start.4
  665.6 2.4 collective-permute-start.5
  668.0 0.9 collective-permute-done.4
  668.9 7.9 collective-permute-done.5
  677.1 0.3 copy.59
  677.5 18.4 %all_to_all.67 = f32[4,128,160]{2,0,1:T(4,128)S(1)} all-to-all(f32[4,128,160]{2,0,1:T(4,128)S(1)} %copy.59), channel_id=1, replica_groups=mesh['chan'=64,'facet'=8] {'chan'}, dimensions={1} | all-to-all | bytes 655360 | tf_op jit(solution)/shard_map/all_to_all | solution.py:97
  696.2 0.4 reshape.46
  696.6 1.3 fusion.31
  698.7 530.9 %all-reduce.11.cloned.1.call-done = f32[256,256]{1,0:T(8,128)} async-done(((f32[256,256]{1,0:T(8,128)}), f32[256,256]{1,0:T(8,128)}) %all-reduce.11.cloned.1.call-update) | async-done | bytes 262160 | tf_op jit(solution)/shard_map/psum | solution.py:45
  1229.6 1.7 select_reduce_fusion
  1231.9 0.3 fusion.3
  1232.6 0.4 fusion.15
  1233.0 0.4 fusion.2
  1233.3 0.4 fusion.1
  1233.7 0.5 fusion.32
  1234.4 22.2 %all_to_all.68 = f32[256,2,160]{2,1,0:T(2,128)S(1)} all-to-all(f32[256,2,160]{2,1,0:T(2,128)S(1)} %copy.62), channel_id=1, replica_groups=mesh['chan'=64,'facet'=8] {'chan'}, dimensions={0} | all-to-all | bytes 655360 | tf_op jit(solution)/shard_map/all_to_all | solution.py:99
  1257.0 35.2 %collective-permute-start.6 = (f32[4,128,16]{2,1,0:T(8,128)S(1)}, f32[4,128,16]{2,1,0:T(8,128)S(1)}, u32[]{:S(2)}, u32[]{:S(2)}) collective-permute-start(f32[4,128,16]{2,1,0:T(8,128)S(1)} %get-tuple-element.5), channel_id=1, source_target_pairs={{0,1},{1,2},{2,3},{3,4},{4,5},{5,6},{6,7},{8,9},{9,10},{10,11},{11... | collective-permute-start | bytes 98312 | tf_op jit(solution)/shard_map/ppermute | solution.py:19
  1292.2 1.9 collective-permute-start.7
  1294.1 1.4 collective-permute-done.6
  1295.5 8.1 collective-permute-done.7
  1303.6 0.9 fusion.9
  (40 shorter events, 3.9 us)
Async XLA Ops:
  6.5 581.7 %all-reduce.9.cloned.1.call-start = ((), (), s32[]{:S(2)}) async-start(), calls=%async_computation.4 | async-start | bytes 524288 | tf_op jit(solution)/shard_map/psum | solution.py:45
  7.8 12.7 collective-permute-start
  13.4 11.4 collective-permute-start.1
  17.9 0.7 copy-start.5
  54.3 0.7 copy-start.6
  588.3 2.3 copy-start.3
  593.9 22.4 %all-to-all-start.1 = ((f32[256,2,160]{2,1,0:T(2,128)}), f32[256,2,160]{2,1,0:T(2,128)S(1)}, u32[]{:S(2)}, u32[]{:S(2)}) async-start(f32[256,2,160]{2,1,0:T(2,128)} %copy.56), calls=%async_computation.1 | async-start | bytes 1048576 | tf_op jit(solution)/shard_map/all_to_all | solution.py:99
  603.1 0.7 copy-start.4
  603.1 626.5 %all-reduce.11.cloned.1.call-start = ((), (), s32[]{:S(2)}) async-start(), calls=%async_computation.5 | async-start | bytes 524288 | tf_op jit(solution)/shard_map/psum | solution.py:45
  616.6 46.7 %copy-start = (f32[4,128,128]{2,1,0:T(8,128)S(1)}, f32[4,128,128]{2,1,0:T(8,128)}, u32[]{:S(2)}) copy-start(f32[4,128,128]{2,1,0:T(8,128)} %param.8) | copy-start | bytes 786436
  616.6 46.7 %copy-start.1 = (f32[4,128,128]{2,1,0:T(8,128)S(1)}, f32[4,128,128]{2,1,0:T(8,128)}, u32[]{:S(2)}) copy-start(f32[4,128,128]{2,1,0:T(8,128)} %param.7) | copy-start | bytes 786436
  616.7 38.5 %collective-permute-start.2 = (f32[4,128,16]{2,1,0:T(8,128)S(1)}, f32[4,128,16]{2,1,0:T(8,128)S(1)}, u32[]{:S(2)}, u32[]{:S(2)}) collective-permute-start(f32[4,128,16]{2,1,0:T(8,128)S(1)} %get-tuple-element.7), channel_id=1, source_target_pairs={{0,1},{1,2},{2,3},{3,4},{4,5},{5,6},{6,7},{8,9},{9,10},{10,11},{11... | collective-permute-start | bytes 98312 | tf_op jit(solution)/shard_map/ppermute | solution.py:19
  651.9 11.4 collective-permute-start.3
  663.6 5.3 collective-permute-start.4
  665.6 11.3 collective-permute-start.5
  1229.6 2.3 copy-start.2
  1257.0 38.5 %collective-permute-start.6 = (f32[4,128,16]{2,1,0:T(8,128)S(1)}, f32[4,128,16]{2,1,0:T(8,128)S(1)}, u32[]{:S(2)}, u32[]{:S(2)}) collective-permute-start(f32[4,128,16]{2,1,0:T(8,128)S(1)} %get-tuple-element.5), channel_id=1, source_target_pairs={{0,1},{1,2},{2,3},{3,4},{4,5},{5,6},{6,7},{8,9},{9,10},{10,11},{11... | collective-permute-start | bytes 98312 | tf_op jit(solution)/shard_map/ppermute | solution.py:19
  1292.2 11.4 collective-permute-start.7
Sparse Core Ops, SparseCore 0:
  54.4 533.8 all-reduce.8
  698.1 531.4 all-reduce.10
where the time goes:
time: 1310 us
  waiting for transfers between devices  1110 us (85%)
  starting transfers between devices  97.7 us (7%)
  blocking collectives  67.4 us (5%)
  between operations  18.3 us (1%)
    psum x2, waiting for transfers between devices, shrink_block(): gram = lax.psum(partial_value, 'chan')  1060 us
    ppermute x4, starting transfers between devices, padded(): before = lax.ppermute(last, axis, up)  77.8 us
    all_to_all x2, blocking collectives, per_device(): lax.all_to_all(extended, 'chan', split_axis=1, concat_axis=0, tiled=True)  45.2 us
    ppermute x4, waiting for transfers between devices, padded(): after = lax.ppermute(initial, axis, down)  28.3 us
  transfers between devices with their start and end apart: 11, of which 10 were waited for; matrix products, arithmetic and copies ran while one was open for 0% of the time, Pallas kernels for 0%

commit v1 on v0

--- a/solution.py
+++ b/solution.py
@@ -3,6 +3,7 @@
 import jax.numpy as jnp
 from jax import lax
 from jax.sharding import PartitionSpec as P
+from jax.lax import all_gather
 
 OV = 16
 NS_STEPS = 2
@@ -42,7 +43,7 @@
 def shrink_block(block, tau_value):
     columns = block.reshape(block.shape[0], -1)
     partial_value = jnp.dot(columns, columns.T, precision=lax.Precision.HIGHEST)
-    gram = lax.psum(partial_value, "chan")
+    gram = all_gather(partial_value, "chan").sum(axis=0)
     return apply_shrink(gram, columns, tau_value).reshape(block.shape)
 
 

time: 1310 us -> 856 us (0.65)
  waiting for transfers between devices: 1110 us -> 616 us
  starting transfers between devices: 97.7 us -> 123 us
    psum x2 -> x0, waiting for transfers between devices: 1060 us -> none  [shrink_block(): gram = lax.psum(partial_value, 'chan')]
    all_gather x0 -> x2, waiting for transfers between devices: none -> 572 us  [shrink_block(): gram = all_gather(partial_value, 'chan').sum(axis=0)]
    ppermute x4, starting transfers between devices: 77.8 us -> 105 us  [padded(): before = lax.ppermute(last, axis, up)]
    reduce_sum x0 -> x2, other arithmetic: none -> 13.7 us  [shrink_block(): gram = all_gather(partial_value, 'chan').sum(axis=0)]
where the time goes in v1:
time: 856 us; the launch traced here: 855 us
  waiting for transfers between devices  616 us (72%)
  starting transfers between devices  123 us (14%)
  blocking collectives  65 us (8%)
  other arithmetic  18.6 us (2%)
  between operations  18.2 us (2%)
    all_gather x2, waiting for transfers between devices, shrink_block(): gram = all_gather(partial_value, 'chan').sum(axis=0)  572 us
    ppermute x4, starting transfers between devices, padded(): before = lax.ppermute(last, axis, up)  105 us
    all_to_all x2, blocking collectives, per_device(): lax.all_to_all(extended, 'chan', split_axis=1, concat_axis=0, tiled=True)  46.7 us
    ppermute x4, waiting for transfers between devices, padded(): after = lax.ppermute(initial, axis, down)  27.7 us
    all_to_all x1, blocking collectives, per_device(): lax.all_to_all(result, 'chan', split_axis=0, concat_axis=1, tiled=True)  18.3 us
  transfers between devices with their start and end apart: 11, of which 10 were waited for; matrix products, arithmetic and copies ran while one was open for 0% of the time, Pallas kernels for 0%

profile of v1, /device:TPU:1, one launch (start us, length us, event | category | flops | bytes accessed | tf_op | source)
XLA Modules:
  0.0 854.9 jit_solution(7561027718314809898)
XLA Ops:
  6.5 1.1 multiply_subtract_fusion.1
  7.8 5.6 collective-permute-start
  13.4 4.5 collective-permute-start.1
  17.9 1.4 fusion.28
  20.6 4.2 collective-permute-done.1
  25.1 0.3 copy.53
  25.5 26.9 %all_to_all.66 = f32[4,128,160]{2,0,1:T(4,128)S(1)} all-to-all(f32[4,128,160]{2,0,1:T(4,128)S(1)} %copy.53), channel_id=1, replica_groups=mesh['chan'=64,'facet'=8] {'chan'}, dimensions={1} | all-to-all | bytes 655360 | tf_op jit(solution)/shard_map/all_to_all | solution.py:98
  52.7 0.4 reshape.45
  53.1 1.3 fusion.29
  54.5 1.4 fusion.27
  56.6 285.9 %all-gather.5.cloned.1.call-done = f32[16384,256]{1,0:T(8,128)} async-done(((f32[256,256]{1,0:T(8,128)}), f32[16384,256]{1,0:T(8,128)}) %all-gather.5.cloned.1.call-update) | async-done | bytes 16777232 | tf_op jit(solution)/shard_map/all_gather | solution.py:46
  342.5 6.8 reduce_sum.34
  349.3 0.6 select_reduce_fusion.1
  350.6 0.3 fusion.7
  351.0 0.4 fusion.14
  351.6 0.4 fusion.6
  352.0 0.4 fusion.5
  352.4 0.5 fusion.30
  352.9 1.0 copy.56
  353.9 7.0 all-to-all-start.1
  361.7 12.8 %all-to-all-done.1 = f32[256,2,160]{2,1,0:T(2,128)S(1)} async-done(((f32[256,2,160]{2,1,0:T(2,128)}), f32[256,2,160]{2,1,0:T(2,128)S(1)}, u32[]{:S(2)}, u32[]{:S(2)}) %all-to-all-start.1) | async-done | bytes 327712 | tf_op jit(solution)/shard_map/all_to_all | solution.py:100
  374.9 48.4 %collective-permute-start.2 = (f32[4,128,16]{2,1,0:T(8,128)S(1)}, f32[4,128,16]{2,1,0:T(8,128)S(1)}, u32[]{:S(2)}, u32[]{:S(2)}) collective-permute-start(f32[4,128,16]{2,1,0:T(8,128)S(1)} %get-tuple-element.7), channel_id=1, source_target_pairs={{0,1},{1,2},{2,3},{3,4},{4,5},{5,6},{6,7},{8,9},{9,10},{10,11},{11... | collective-permute-start | bytes 98312 | tf_op jit(solution)/shard_map/ppermute | solution.py:20
  423.3 1.9 collective-permute-start.3
  425.2 0.6 fusion.17
  425.9 0.8 collective-permute-done.2
  426.7 8.1 collective-permute-done.3
  435.1 1.9 collective-permute-start.4
  437.0 2.4 collective-permute-start.5
  439.4 0.9 collective-permute-done.4
  440.3 7.4 collective-permute-done.5
  448.0 0.3 copy.59
  448.3 19.7 %all_to_all.67 = f32[4,128,160]{2,0,1:T(4,128)S(1)} all-to-all(f32[4,128,160]{2,0,1:T(4,128)S(1)} %copy.59), channel_id=1, replica_groups=mesh['chan'=64,'facet'=8] {'chan'}, dimensions={1} | all-to-all | bytes 655360 | tf_op jit(solution)/shard_map/all_to_all | solution.py:98
  468.3 0.4 reshape.46
  468.8 1.3 fusion.31
  470.9 286.1 %all-gather.7.cloned.1.call-done = f32[16384,256]{1,0:T(8,128)} async-done(((f32[256,256]{1,0:T(8,128)}), f32[16384,256]{1,0:T(8,128)}) %all-gather.7.cloned.1.call-update) | async-done | bytes 16777232 | tf_op jit(solution)/shard_map/all_gather | solution.py:46
  757.0 6.8 reduce_sum.36
  763.8 0.6 select_reduce_fusion
  765.1 0.3 fusion.3
  765.4 0.4 fusion.15
  766.1 0.4 fusion.2
  766.5 0.4 fusion.1
  766.9 0.5 fusion.32
  767.6 18.3 %all_to_all.68 = f32[256,2,160]{2,1,0:T(2,128)S(1)} all-to-all(f32[256,2,160]{2,1,0:T(2,128)S(1)} %copy.62), channel_id=1, replica_groups=mesh['chan'=64,'facet'=8] {'chan'}, dimensions={0} | all-to-all | bytes 655360 | tf_op jit(solution)/shard_map/all_to_all | solution.py:100
  786.3 49.4 %collective-permute-start.6 = (f32[4,128,16]{2,1,0:T(8,128)S(1)}, f32[4,128,16]{2,1,0:T(8,128)S(1)}, u32[]{:S(2)}, u32[]{:S(2)}) collective-permute-start(f32[4,128,16]{2,1,0:T(8,128)S(1)} %get-tuple-element.5), channel_id=1, source_target_pairs={{0,1},{1,2},{2,3},{3,4},{4,5},{5,6},{6,7},{8,9},{9,10},{10,11},{11... | collective-permute-start | bytes 98312 | tf_op jit(solution)/shard_map/ppermute | solution.py:20
  835.7 1.9 collective-permute-start.7
  837.6 1.4 collective-permute-done.6
  839.1 8.1 collective-permute-done.7
  847.1 0.9 fusion.9
  (34 shorter events, 3.5 us)
Async XLA Ops:
  6.5 335.9 %all-gather.5.cloned.1.call-start = ((), (), s32[]{:S(2)}) async-start(), calls=%async_computation.4 | async-start | bytes 17039360 | tf_op jit(solution)/shard_map/all_gather | solution.py:46
  7.7 353.2 %copy-start.2 = (s32[8,160]{1,0:T(8,128)S(1)}, s32[8,160]{1,0:T(8,128)}, u32[]{:S(2)}) copy-start(s32[8,160]{1,0:T(8,128)} %param.10) | copy-start | bytes 15364
  7.8 12.8 %collective-permute-start = (f32[4,128,16]{2,1,0:T(8,128)S(1)}, f32[4,128,16]{2,1,0:T(8,128)S(1)}, u32[]{:S(2)}, u32[]{:S(2)}) collective-permute-start(f32[4,128,16]{2,1,0:T(8,128)S(1)} %get-tuple-element.11), channel_id=1, source_target_pairs={{0,1},{1,2},{2,3},{3,4},{4,5},{5,6},{6,7},{8,9},{9,10},{10,11},{11... | collective-permute-start | bytes 98312 | tf_op jit(solution)/shard_map/ppermute | solution.py:20
  13.4 11.4 %collective-permute-start.1 = (f32[4,128,16]{2,1,0:T(8,128)S(1)}, f32[4,128,16]{2,1,0:T(8,128)S(1)}, u32[]{:S(2)}, u32[]{:S(2)}) collective-permute-start(f32[4,128,16]{2,1,0:T(8,128)S(1)} %get-tuple-element.12), channel_id=1, source_target_pairs={{1,0},{2,1},{3,2},{4,3},{5,4},{6,5},{7,6},{9,8},{10,9},{11,10},{12... | collective-permute-start | bytes 98312 | tf_op jit(solution)/shard_map/ppermute | solution.py:21
  25.5 409.2 %copy-start = (f32[4,128,128]{2,1,0:T(8,128)S(1)}, f32[4,128,128]{2,1,0:T(8,128)}, u32[]{:S(2)}) copy-start(f32[4,128,128]{2,1,0:T(8,128)} %param.8) | copy-start | bytes 786436
  25.5 409.2 %copy-start.1 = (f32[4,128,128]{2,1,0:T(8,128)S(1)}, f32[4,128,128]{2,1,0:T(8,128)}, u32[]{:S(2)}) copy-start(f32[4,128,128]{2,1,0:T(8,128)} %param.7) | copy-start | bytes 786436
  353.9 20.6 %all-to-all-start.1 = ((f32[256,2,160]{2,1,0:T(2,128)}), f32[256,2,160]{2,1,0:T(2,128)S(1)}, u32[]{:S(2)}, u32[]{:S(2)}) async-start(f32[256,2,160]{2,1,0:T(2,128)} %copy.56), calls=%async_computation.1 | async-start | bytes 1048576 | tf_op jit(solution)/shard_map/all_to_all | solution.py:100
  360.9 396.1 %all-gather.7.cloned.1.call-start = ((), (), s32[]{:S(2)}) async-start(), calls=%async_computation.5 | async-start | bytes 17039360 | tf_op jit(solution)/shard_map/all_gather | solution.py:46
  374.9 51.8 %collective-permute-start.2 = (f32[4,128,16]{2,1,0:T(8,128)S(1)}, f32[4,128,16]{2,1,0:T(8,128)S(1)}, u32[]{:S(2)}, u32[]{:S(2)}) collective-permute-start(f32[4,128,16]{2,1,0:T(8,128)S(1)} %get-tuple-element.7), channel_id=1, source_target_pairs={{0,1},{1,2},{2,3},{3,4},{4,5},{5,6},{6,7},{8,9},{9,10},{10,11},{11... | collective-permute-start | bytes 98312 | tf_op jit(solution)/shard_map/ppermute | solution.py:20
  423.3 11.4 %collective-permute-start.3 = (f32[4,128,16]{2,1,0:T(8,128)S(1)}, f32[4,128,16]{2,1,0:T(8,128)S(1)}, u32[]{:S(2)}, u32[]{:S(2)}) collective-permute-start(f32[4,128,16]{2,1,0:T(8,128)S(1)} %get-tuple-element.8), channel_id=1, source_target_pairs={{1,0},{2,1},{3,2},{4,3},{5,4},{6,5},{7,6},{9,8},{10,9},{11,10},{12... | collective-permute-start | bytes 98312 | tf_op jit(solution)/shard_map/ppermute | solution.py:21
  435.1 5.3 collective-permute-start.4
  437.0 10.7 %collective-permute-start.5 = (f32[4,128,16]{2,1,0:T(8,128)S(1)}, f32[4,128,16]{2,1,0:T(8,128)S(1)}, u32[]{:S(2)}, u32[]{:S(2)}) collective-permute-start(f32[4,128,16]{2,1,0:T(8,128)S(1)} %get-tuple-element.10), channel_id=1, source_target_pairs={{1,0},{2,1},{3,2},{4,3},{5,4},{6,5},{7,6},{9,8},{10,9},{11,10},{12... | collective-permute-start | bytes 98312 | tf_op jit(solution)/shard_map/ppermute | solution.py:21
  786.3 52.8 %collective-permute-start.6 = (f32[4,128,16]{2,1,0:T(8,128)S(1)}, f32[4,128,16]{2,1,0:T(8,128)S(1)}, u32[]{:S(2)}, u32[]{:S(2)}) collective-permute-start(f32[4,128,16]{2,1,0:T(8,128)S(1)} %get-tuple-element.5), channel_id=1, source_target_pairs={{0,1},{1,2},{2,3},{3,4},{4,5},{5,6},{6,7},{8,9},{9,10},{10,11},{11... | collective-permute-start | bytes 98312 | tf_op jit(solution)/shard_map/ppermute | solution.py:20
  835.7 11.4 %collective-permute-start.7 = (f32[4,128,16]{2,1,0:T(8,128)S(1)}, f32[4,128,16]{2,1,0:T(8,128)S(1)}, u32[]{:S(2)}, u32[]{:S(2)}) collective-permute-start(f32[4,128,16]{2,1,0:T(8,128)S(1)} %get-tuple-element.6), channel_id=1, source_target_pairs={{1,0},{2,1},{3,2},{4,3},{5,4},{6,5},{7,6},{9,8},{10,9},{11,10},{12... | collective-permute-start | bytes 98312 | tf_op jit(solution)/shard_map/ppermute | solution.py:21
Sparse Core Ops, SparseCore 0:
  54.6 287.8 all-gather.4
  470.2 286.6 all-gather.6
